TPU v7x, 32 devices: a whole 2x2x4 slice. The times are simulated.
32 devices in a mesh: lat: 4 (over x, core), lon: 8 (over z, y).
Axes of the slice: x: 2, y: 2, z: 4, core: 2. Of those that a mesh axis runs over, the one named last changes fastest.
Arguments:
- spectra: bfloat16 [98304, 616], P(('lat', 'lon')), may hold values from -6 to 6
- block_target: int32 [768], P(('lat', 'lon')), may hold values from 0 to 7, as said below
- block_patch: int32 [768], P(('lat', 'lon')), may hold values from 0 to 11
- block_kernel: int32 [768], P(('lat', 'lon')), may hold values from 0 to 15
- encoder_weight: bfloat16 [616, 512], replicated, may hold values from -0.25 to 0.25
- kernels: bfloat16 [16, 128, 128], replicated, may hold values from 0.049804688 to 1
- gain: float32 [512], replicated, may hold values from 0.1 to 1.9
- conv_weight: bfloat16 [3, 3, 512, 512], replicated, may hold values from -0.09375 to 0.09375
- cotangent: bfloat16 [96, 512, 512], P('lat', 'lon'), may hold values from -6 to 6
Outputs:
- conv_out: bfloat16 [96, 512, 512], P('lat', 'lon')
- conv_grad: float32 [3, 3, 512, 512], replicated
- encoder_grad: float32 [616, 512], replicated
- gain_grad: float32 [512], replicated
Inputs may be any that keep to these rules, and one draw needn't show every extreme that they name: `block_target`: within one device's 24 blocks no tile is named more than 3 times; in every latitude band one tile is named exactly 3 times by every device of the band.
All inputs are finite; a program needn't handle non-finite values.
Results may differ from a plain program's by a relative error of at most 0.0059.
Values may be sent and summed in bfloat16 or wider, within the bound.
No kernel may reach another device: no remote copies, remote signals or barrier semaphores. Data moves between devices by JAX's collectives and lax.ppermute only.
A program may use at most 192 MiB of HBM per device.

v0:
```python
import math
import jax
import jax.numpy as jnp
from jax import lax
from jax.sharding import PartitionSpec as P

PH = 8
PW = 16
MOST = 3


def padded_2(shard, sides, width, wrap):
    for axis, dim in sides:
        size, length = (lax.axis_size(axis), shard.shape[dim])
        up = [(i, (i + 1) % size) for i in range(size if wrap else size - 1)]
        down = [(j, i) for i, j in up]
        last = lax.slice_in_dim(shard, length - width, length, axis=dim)
        leading = lax.slice_in_dim(shard, 0, width, axis=dim)
        before = lax.ppermute(last, axis, up)
        after = lax.ppermute(leading, axis, down)
        shard = jnp.concatenate([before, shard, after], axis=dim)
    return shard


def normalise(field, gain):
    meansq = jnp.mean(field * field, axis=-1, keepdims=True)
    return field * lax.rsqrt(meansq + 1e-06) * gain


def silu_slope(preact):
    logistic = jax.nn.sigmoid(preact)
    return logistic * (1.0 + preact * (1.0 - logistic))


def widen(field):
    beside_all = padded_2(field, (("lon", 1),), 1, True)
    return padded_2(beside_all, (("lat", 0),), 1, False)


def slot_layout(targets, lon_count):
    lanes = jnp.arange(lon_count, dtype=jnp.int32)
    onehot = (targets[..., None] == lanes).astype(jnp.int32)
    before = jnp.cumsum(onehot, axis=-2) - onehot
    ranks = jnp.sum(before * onehot, axis=-1)
    return targets * MOST + ranks


def to_tile(patches_in, tile_rows, tile_cols, width):
    shaped = patches_in.reshape(tile_rows // PH, tile_cols // PW, PH, PW, width)
    return shaped.transpose(0, 2, 1, 3, 4).reshape(tile_rows, tile_cols, width)


def to_patches(tile, tile_rows, tile_cols, width):
    shaped = tile.reshape(tile_rows // PH, PH, tile_cols // PW, PW, width)
    return shaped.transpose(0, 2, 1, 3, 4).reshape(-1, PH * PW, width)


def shards(
    spectra,
    block_target,
    block_patch,
    block_kernel,
    encoder_weight,
    kernels,
    gain,
    conv_weight,
    cotangent,
):
    lon_count = lax.axis_size("lon")
    lat_count = lax.axis_size("lat")
    own_lon = lax.axis_index("lon")
    blocks = block_target.shape[0]
    kernel_count, block_rows, patch_cells = kernels.shape
    channels = spectra.shape[1]
    width = encoder_weight.shape[1]
    tile_rows, tile_cols = (cotangent.shape[0], cotangent.shape[1])
    slots = lon_count * MOST
    patch_count = tile_rows // PH * (tile_cols // PW)
    loss_scale = 1.0 / math.sqrt(tile_rows * lat_count * tile_cols * lon_count)
    all_target, all_patch, all_kernel = (
        lax.all_gather(block_target, "lon", axis=0, tiled=True),
        lax.all_gather(block_patch, "lon", axis=0, tiled=True),
        lax.all_gather(block_kernel, "lon", axis=0, tiled=True),
    )
    all_target = all_target.reshape(lon_count, blocks)
    all_patch = all_patch.reshape(lon_count, blocks)
    all_kernel = all_kernel.reshape(lon_count, blocks)
    own_slot = slot_layout(block_target, lon_count)
    slot_ids = jnp.arange(slots, dtype=jnp.int32)
    chosen_slots = own_slot[None, :] == slot_ids[:, None]
    filled = jnp.any(chosen_slots, axis=1)
    source_block = jnp.sum(chosen_slots * jnp.arange(blocks, dtype=jnp.int32)[None, :], axis=1)
    all_slot = slot_layout(all_target, lon_count)
    wanted = own_lon * MOST + jnp.arange(MOST, dtype=jnp.int32)
    arrive = (all_slot[:, None, :] == wanted[None, :, None]).astype(jnp.int32)
    present = jnp.sum(arrive, axis=2).reshape(-1) > 0
    slot_kernel = jnp.sum(arrive * all_kernel[:, None, :], axis=2).reshape(-1)
    slot_kernel = jnp.where(present, slot_kernel, -1)
    slot_patch = jnp.sum(arrive * all_patch[:, None, :], axis=2).reshape(-1)
    taken = jnp.take(spectra.reshape(blocks, block_rows, channels), source_block, axis=0)
    taken = jnp.where(filled[:, None, None], taken, jnp.zeros_like(taken))
    arrived = lax.all_to_all(
        taken.reshape(lon_count, MOST, -1), "lon", split_axis=0, concat_axis=0, tiled=True
    )
    slot_spectra = arrived.reshape(slots * block_rows, channels)
    slot_preact = jnp.dot(slot_spectra, encoder_weight, preferred_element_type=jnp.float32)
    slot_rows = jax.nn.silu(slot_preact).astype(jnp.bfloat16).reshape(slots, block_rows, width)
    kernel_pick = (
        slot_kernel[:, None] == jnp.arange(kernel_count, dtype=jnp.int32)[None, :]
    ).astype(jnp.bfloat16)
    slot_kernels = jnp.dot(
        kernel_pick, kernels.reshape(kernel_count, -1), preferred_element_type=jnp.float32
    )
    slot_kernels = slot_kernels.astype(jnp.bfloat16).reshape(slots, block_rows, patch_cells)
    contribution = jnp.einsum(
        "sbp,sbd->spd", slot_kernels, slot_rows, preferred_element_type=jnp.float32
    )
    patch_pick = (slot_patch[:, None] == jnp.arange(patch_count, dtype=jnp.int32)[None, :]).astype(
        jnp.float32
    )
    tile_patches = jnp.einsum(
        "sq,spd->qpd", patch_pick, contribution, precision=lax.Precision.HIGHEST
    )
    spread = to_tile(tile_patches, tile_rows, tile_cols, width)
    normed = normalise(spread, gain).astype(jnp.bfloat16)
    padded = widen(normed)
    windows = []
    result_sum = jnp.zeros((tile_rows * tile_cols, width), jnp.float32)
    for row_shift in range(3):
        for col_shift in range(3):
            window = padded[
                row_shift : row_shift + tile_rows, col_shift : col_shift + tile_cols
            ].reshape(-1, width)
            windows.append(window)
            result_sum = result_sum + jnp.dot(
                window, conv_weight[row_shift, col_shift], preferred_element_type=jnp.float32
            )
    conv_out = result_sum.reshape(tile_rows, tile_cols, width).astype(jnp.bfloat16)
    cot_padded = widen(cotangent)
    cot_flat = cotangent.reshape(-1, width)
    d_normed = jnp.zeros((tile_rows * tile_cols, width), jnp.float32)
    kernel_grads = []
    for row_shift in range(3):
        for col_shift in range(3):
            back_window = cot_padded[
                2 - row_shift : 2 - row_shift + tile_rows, 2 - col_shift : 2 - col_shift + tile_cols
            ].reshape(-1, width)
            d_normed = d_normed + lax.dot_general(
                back_window,
                conv_weight[row_shift, col_shift],
                (((1,), (1,)), ((), ())),
                preferred_element_type=jnp.float32,
            )
            kernel_grads.append(
                lax.dot_general(
                    windows[row_shift * 3 + col_shift],
                    cot_flat,
                    (((0,), (0,)), ((), ())),
                    preferred_element_type=jnp.float32,
                )
            )
    conv_part = jnp.stack(kernel_grads).reshape(3, 3, width, width)
    _, pullback = jax.vjp(normalise, spread, gain)
    d_spread, gain_part = pullback(d_normed.reshape(tile_rows, tile_cols, width))
    d_patches = to_patches(d_spread.astype(jnp.bfloat16), tile_rows, tile_cols, width)
    slot_dpatch = jnp.take(d_patches, slot_patch, axis=0)
    slot_drows = jnp.einsum(
        "sbp,spd->sbd", slot_kernels, slot_dpatch, preferred_element_type=jnp.float32
    ).astype(jnp.bfloat16)
    d_preact = (slot_drows.reshape(-1, width).astype(jnp.float32) * silu_slope(slot_preact)).astype(
        jnp.bfloat16
    )
    encoder_part = lax.dot_general(
        slot_spectra, d_preact, (((0,), (0,)), ((), ())), preferred_element_type=jnp.float32
    )
    conv_total, encoder_total, gain_total = lax.psum(
        (conv_part, encoder_part, gain_part), ("lat", "lon")
    )
    return (conv_out, conv_total * loss_scale, encoder_total * loss_scale, gain_total * loss_scale)


def solution(mesh):
    placed = (
        P(("lat", "lon"), None),
        P(("lat", "lon")),
        P(("lat", "lon")),
        P(("lat", "lon")),
        P(),
        P(),
        P(),
        P(),
        P("lat", "lon", None),
    )
    return jax.shard_map(
        shards,
        mesh=mesh,
        in_specs=placed,
        out_specs=(P("lat", "lon", None), P(), P(), P()),
        check_vma=False,
    )
```

profile of v0, /device:TPU:0, one launch (start us, length us, event | category | flops | bytes accessed | tf_op | source)
XLA Modules:
  0.0 510.4 jit_solution(6960326215886359969)
XLA Ops:
  14.3 13.1 %all-reduce.3 = (s32[192]{0:T(256)S(1)}, s32[192]{0:T(256)S(1)}, s32[192]{0:T(256)S(1)}) all-reduce(s32[192]{0:T(256)S(1)} %dynamic-update-slice.1, s32[192]{0:T(256)S(1)} %dynamic-update-slice, s32[192]{0:T(256)S(1)} %dynamic-update-slice.2), channel_id=1, replica_groups=mesh['lat'=4,'lon'=8] {'lon'}, use_global_device_ids=true, to_apply=%add.1 | all-reduce | flops 576 | bytes 4608
  29.1 4.6 copy_bitcast_fusion
  33.7 5.1 gather_fusion
  38.8 6.2 %copy.96 = bf16[24,128,616]{2,1,0:T(8,128)(2,1)} copy(bf16[24,128,616]{1,2,0:T(8,128)(2,1)} %gather_fusion) | data formatting | bytes 7569408 | tf_op jit(solution)/shard_map/jit(_take)/gather | solution.py:100
  45.1 10.8 %gather.11 = bf16[8,3,78848]{2,1,0:T(4,128)(2,1)} reshape(bf16[24,128,616]{2,1,0:T(8,128)(2,1)} %copy.96) | data formatting | bytes 7569408 | tf_op jit(solution)/shard_map/jit(_take)/gather | solution.py:100
  55.9 7.2 %select_select_fusion = bf16[8,3,78848]{2,1,0:T(4,128)(2,1)} fusion(bf16[8,3,78848]{2,1,0:T(4,128)(2,1)} %gather.11, pred[8,3]{1,0:T(8,128)(4,1)S(1)} %copy.94, pred[8,3]{1,0:T(8,128)(4,1)S(1)} %broadcast_in_dim.57), kind=kLoop, calls=%fused_computation.9 | loop fusion | flops 3784704 | bytes 7569456 | tf_op jit(solution)/shard_map/jit(_where)/select_n | solution.py:101
  63.1 4.8 all-to-all-start
  69.9 2.9 collective-permute-start.5
  73.0 2.1 fusion.41
  75.8 76.7 %collective-permute-done.4 = bf16[24,1,512]{2,1,0:T(2,128)(2,1)S(1)} collective-permute-done((bf16[24,1,512]{2,1,0:T(2,128)(2,1)S(1)}, bf16[24,1,512]{2,1,0:T(2,128)(2,1)S(1)}, u32[]{:S(2)}, u32[]{:S(2)}) %collective-permute-start.4) | collective-permute-done | bytes 24608 | tf_op jit(solution)/shard_map/ppermute | solution.py:19
  153.9 3.2 collective-permute-start.7
  160.3 2.3 fusion.96
  170.1 2.7 convolution_add_fusion
  172.8 4.4 all-to-all-done
  177.2 10.9 %reshape.259 = bf16[3072,616]{1,0:T(8,128)(2,1)} reshape(bf16[8,3,78848]{2,1,0:T(4,128)(2,1)} %all-to-all-done) | data formatting | bytes 7569408 | tf_op jit(solution)/shard_map/reshape | solution.py:105
  188.0 7.0 %multiply_convert_fusion = (bf16[3072,512]{1,0:T(8,128)(2,1)S(1)}, f32[3072,512]{1,0:T(8,128)}) fusion(bf16[3072,616]{1,0:T(8,128)(2,1)} %reshape.259, bf16[616,512]{1,0:T(8,128)(2,1)S(1)} %copy-done), kind=kOutput, calls=%fused_computation.7 | convolution fusion | flops 1945632768 | bytes 13852672 | tf_op jit(solution)/shard_map/dot_general | solution.py:106
  196.1 6.3 %fusion.1 = f32[12,128,512]{2,0,1:T(8,128)S(1)} fusion(f32[24,128,512]{2,1,0:T(8,128)S(1)} %fusion.101, s32[24]{0:T(128)S(1)} %eq.86), kind=kOutput, calls=%fused_computation.5 | convolution fusion | flops 226492704 | bytes 9437280 | tf_op jit(solution)/shard_map/sq,spd->qpd/dot_general | solution.py:121
  209.1 4.7 fusion.7
  215.4 2.1 collective-permute-start
  217.5 2.9 collective-permute-start.1
  220.3 3.9 gather_fusion.1
  224.3 2.9 fusion.14
  227.2 4.5 fusion
  231.7 3.2 fusion.102
  238.7 2.4 collective-permute-done.3
  252.4 3.7 copy-done.18
  258.9 2.3 fusion.9
  261.2 61.9 %psum.23 = f32[512]{0:T(512)S(1)} all-reduce(f32[512]{0:T(512)S(1)} %fusion.9), channel_id=1, replica_groups=mesh['lat'=4,'lon'=8] {'lat','lon'}, use_global_device_ids=true, to_apply=%region_14.15 | all-reduce | flops 512 | bytes 4096 | tf_op jit(solution)/shard_map/psum | solution.py:176
  323.7 2.7 fusion.43
  337.1 2.1 fusion.13
  339.2 153.7 %all-reduce.7.cloned.1.call-done = (f32[3,3,512,512]{3,2,1,0:T(8,128)}, f32[616,512]{1,0:T(8,128)}) async-done(((f32[3,3,512,512]{3,2,1,0:T(8,128)}, f32[616,512]{1,0:T(8,128)}), (f32[3,3,512,512]{3,2,1,0:T(8,128)}, f32[616,512]{1,0:T(8,128)})) %all-reduce.7.cloned.1.call-update) | async-done | bytes 10698768 | tf_op jit(solution)/shard_map/psum | solution.py:176
  492.9 9.2 %broadcast_multiply_fusion = f32[3,3,512,512]{3,2,1,0:T(8,128)} fusion(f32[3,3,512,512]{3,2,1,0:T(8,128)} %get-tuple-element.12), kind=kLoop, calls=%fused_computation.11 | loop fusion | flops 2359296 | bytes 18874368 | tf_op jit(solution)/shard_map/mul | solution.py:179
  (151 shorter events, 62.3 us)
Async XLA Ops:
  7.2 180.9 %copy-start = (bf16[616,512]{1,0:T(8,128)(2,1)S(1)}, bf16[616,512]{1,0:T(8,128)(2,1)}, u32[]{:S(2)}) copy-start(bf16[616,512]{1,0:T(8,128)(2,1)} %param.13) | copy-start | bytes 1892356
  63.1 4.8 copy-start.2
  63.1 114.1 %all-to-all-start = ((bf16[8,3,78848]{2,1,0:T(4,128)(2,1)}), bf16[8,3,78848]{2,1,0:T(4,128)(2,1)}, u32[]{:S(2)}, u32[]{:S(2)}) async-start(bf16[8,3,78848]{2,1,0:T(4,128)(2,1)} %select_select_fusion), calls=%async_computation | async-start | bytes 10092544 | tf_op jit(solution)/shard_map/all_to_all | solution.py:102
  67.8 425.1 %all-reduce.7.cloned.1.call-start = ((), (), s32[]{:S(2)}) async-start(), calls=%async_computation.1 | async-start | bytes 21397504 | tf_op jit(solution)/shard_map/psum | solution.py:176
  68.0 84.6 %collective-permute-start.4 = (bf16[24,1,512]{2,1,0:T(2,128)(2,1)S(1)}, bf16[24,1,512]{2,1,0:T(2,128)(2,1)S(1)}, u32[]{:S(2)}, u32[]{:S(2)}) collective-permute-start(bf16[24,1,512]{2,1,0:T(2,128)(2,1)S(1)} %get-tuple-element.42), channel_id=1, source_target_pairs={{0,1},{1,2},{2,3},{3,4},{4,5},{5,6},{6,7},{7,0},{8,9},{9,10},{10,1... | collective-permute-start | bytes 73736 | tf_op jit(solution)/shard_map/ppermute | solution.py:19
  69.9 82.7 %collective-permute-start.5 = (bf16[24,1,512]{2,1,0:T(2,128)(2,1)S(1)}, bf16[24,1,512]{2,1,0:T(2,128)(2,1)S(1)}, u32[]{:S(2)}, u32[]{:S(2)}) collective-permute-start(bf16[24,1,512]{2,1,0:T(2,128)(2,1)S(1)} %get-tuple-element.43), channel_id=1, source_target_pairs={{1,0},{2,1},{3,2},{4,3},{5,4},{6,5},{7,6},{0,7},{9,8},{10,9},{11,1... | collective-permute-start | bytes 73736 | tf_op jit(solution)/shard_map/ppermute | solution.py:20
  73.0 2.2 copy-start.21
  152.6 5.6 %collective-permute-start.6 = (bf16[1,66,512]{2,1,0:T(8,128)(2,1)S(1)}, bf16[1,66,512]{2,1,0:T(8,128)(2,1)S(1)}, u32[]{:S(2)}, u32[]{:S(2)}) collective-permute-start(bf16[1,66,512]{2,1,0:T(8,128)(2,1)S(1)} %get-tuple-element.34), channel_id=1, source_target_pairs={{8,0},{16,8},{24,16},{9,1},{17,9},{25,17},{10,2},{18,10},{26,18},{... | collective-permute-start | bytes 202760 | tf_op jit(solution)/shard_map/ppermute | solution.py:20
  153.9 4.3 collective-permute-start.7
  158.2 4.4 slice-start
  160.3 2.4 slice-start.1
  204.2 3.2 copy-start.3
  204.2 4.2 copy-start.4
  204.2 4.2 copy-start.22
  209.1 4.7 copy-start.11
  215.4 19.5 %collective-permute-start = (bf16[24,1,512]{2,1,0:T(2,128)(2,1)S(1)}, bf16[24,1,512]{2,1,0:T(2,128)(2,1)S(1)}, u32[]{:S(2)}, u32[]{:S(2)}) collective-permute-start(bf16[24,1,512]{2,1,0:T(2,128)(2,1)S(1)} %get-tuple-element.38), channel_id=1, source_target_pairs={{0,1},{1,2},{2,3},{3,4},{4,5},{5,6},{6,7},{7,0},{8,9},{9,10},{10,1... | collective-permute-start | bytes 73736 | tf_op jit(solution)/shard_map/ppermute | solution.py:19
  217.5 17.4 %collective-permute-start.1 = (bf16[24,1,512]{2,1,0:T(2,128)(2,1)S(1)}, bf16[24,1,512]{2,1,0:T(2,128)(2,1)S(1)}, u32[]{:S(2)}, u32[]{:S(2)}) collective-permute-start(bf16[24,1,512]{2,1,0:T(2,128)(2,1)S(1)} %get-tuple-element.39), channel_id=1, source_target_pairs={{1,0},{2,1},{3,2},{4,3},{5,4},{6,5},{7,6},{0,7},{9,8},{10,9},{11,1... | collective-permute-start | bytes 73736 | tf_op jit(solution)/shard_map/ppermute | solution.py:20
  227.2 4.5 copy-start.10
  231.7 3.2 copy-start.7
  234.9 3.7 collective-permute-start.2
  236.2 4.9 collective-permute-start.3
  238.7 7.6 %copy-start.16 = (bf16[24,64,512]{2,1,0:T(8,128)(2,1)}, bf16[24,64,512]{2,1,0:T(8,128)(2,1)S(1)}, u32[]{:S(2)}) copy-start(bf16[24,64,512]{2,1,0:T(8,128)(2,1)S(1)} %get-tuple-element.37) | copy-start | bytes 4718596
  238.7 9.6 %copy-start.14 = (bf16[24,64,512]{2,1,0:T(8,128)(2,1)}, bf16[24,64,512]{2,1,0:T(8,128)(2,1)S(1)}, u32[]{:S(2)}) copy-start(bf16[24,64,512]{2,1,0:T(8,128)(2,1)S(1)} %get-tuple-element.36) | copy-start | bytes 4718596
  243.2 2.1 copy-start.12
  243.2 8.2 %copy-start.8 = (bf16[25,66,512]{2,1,0:T(8,128)(2,1)}, bf16[25,66,512]{2,1,0:T(8,128)(2,1)S(1)}, u32[]{:S(2)}) copy-start(bf16[25,66,512]{2,1,0:T(8,128)(2,1)S(1)} %get-tuple-element.29) | copy-start | bytes 5068804
  252.4 3.7 copy-start.18
  256.3 2.6 copy-start.5
  323.7 2.7 copy-start.13
  323.7 3.8 slice-start.2
  327.6 1.5 copy-start.9
  492.9 9.2 %copy-start.20 = (f32[616,512]{1,0:T(8,128)S(1)}, f32[616,512]{1,0:T(8,128)}, u32[]{:S(2)}) copy-start(f32[616,512]{1,0:T(8,128)} %get-tuple-element.13) | copy-start | bytes 3784708
  492.9 10.4 %copy-start.1 = (bf16[616,512]{1,0:T(8,128)(2,1)S(1)}, bf16[616,512]{1,0:T(8,128)(2,1)}, u32[]{:S(2)}) copy-start(bf16[616,512]{1,0:T(8,128)(2,1)} %param.13) | copy-start | bytes 1892356
  (5 other events, 6.7 us)
Sparse Core Ops, SparseCore 0:
  256.3 236.5 all-reduce.6
where the time goes:
time: 518 us; the launch traced here: 510 us
  waiting for transfers between devices  237 us (46%)
  blocking collectives  75 us (14%)
  local copies, waits for them, and re-layouts  66.4 us (13%)
  matrix products  54.1 us (10%)
  other arithmetic  40.5 us (8%)
  starting transfers between devices  21.6 us (4%)
  between operations  15.6 us (3%)
    psum x1, waiting for transfers between devices, shards(): lax.psum((conv_part, encoder_part, gain_part), ('lat', 'lon'))  154 us
    ppermute x4, waiting for transfers between devices, padded_2(): before = lax.ppermute(last, axis, up)  76.7 us
    psum x1, blocking collectives, shards(): lax.psum((conv_part, encoder_part, gain_part), ('lat', 'lon'))  61.9 us
    gather x3, local copies, waits for them, and re-layouts, shards(): jnp.take(spectra.reshape(blocks, block_rows, channels), source_block, axi...  22.1 us
    unnamed x62, local copies, waits for them, and re-layouts  13.8 us
    unnamed x1, blocking collectives  13.1 us
    dot_general x9, matrix products, shards(): lax.dot_general(back_window, conv_weight[row_shift, col_shift], (((1,), (...  12.2 us
    dot_general x9, matrix products, shards(): jnp.dot(window, conv_weight[row_shift, col_shift], preferred_element_type...  11.8 us
  transfers between devices with their start and end apart: 10, of which 4 were waited for; matrix products, arithmetic and copies ran while one was open for 10% of the time, Pallas kernels for 0%

commit v1 on v0

--- a/solution.py
+++ b/solution.py
@@ -1,3 +1,4 @@
+import functools
 import math
 import jax
 import jax.numpy as jnp
@@ -7,6 +8,15 @@
 PH = 8
 PW = 16
 MOST = 3
+
+
+def form_scenes(xin, ax_name, shard_axis):
+    for num in (shard_axis, ax_name):
+        xin = lax.psum(xin, num)
+    return xin
+
+
+_view_strings = functools.partial(form_scenes, ax_name="lat", shard_axis="lon")
 
 
 def padded_2(shard, sides, width, wrap):
@@ -173,9 +183,7 @@
     encoder_part = lax.dot_general(
         slot_spectra, d_preact, (((0,), (0,)), ((), ())), preferred_element_type=jnp.float32
     )
-    conv_total, encoder_total, gain_total = lax.psum(
-        (conv_part, encoder_part, gain_part), ("lat", "lon")
-    )
+    conv_total, encoder_total, gain_total = _view_strings((conv_part, encoder_part, gain_part))
     return (conv_out, conv_total * loss_scale, encoder_total * loss_scale, gain_total * loss_scale)
 
 

time: 518 us -> 828 us (1.60)
  waiting for transfers between devices: 237 us -> 583 us
  blocking collectives: 75 us -> 39 us
    psum x1 -> x2, waiting for transfers between devices: 154 us -> 500 us  [form_scenes(): xin = lax.psum(xin, num)]
    psum x1 -> x2, blocking collectives: 61.9 us -> 25.9 us  [form_scenes(): xin = lax.psum(xin, num)]
  transfers between devices with their start and end apart: 10 -> 11, of which waited for: 4 -> 5; matrix products, arithmetic and copies ran while one was open for 10% -> 6% of each run, Pallas kernels for 0% -> 0%
where the time goes in v1:
time: 828 us; the launch traced here: 820 us
  waiting for transfers between devices  583 us (70%)
  local copies, waits for them, and re-layouts  65.9 us (8%)
  matrix products  53.6 us (6%)
  other arithmetic  40.5 us (5%)
  blocking collectives  39 us (5%)
  starting transfers between devices  21.6 us (3%)
  between operations  15.6 us (2%)
    psum x2, waiting for transfers between devices, form_scenes(): xin = lax.psum(xin, num)  500 us
    ppermute x4, waiting for transfers between devices, padded_2(): before = lax.ppermute(last, axis, up)  76.7 us
    psum x2, blocking collectives, form_scenes(): xin = lax.psum(xin, num)  25.9 us
    gather x3, local copies, waits for them, and re-layouts, shards(): jnp.take(spectra.reshape(blocks, block_rows, channels), source_block, axi...  22 us
  transfers between devices with their start and end apart: 11, of which 5 were waited for; matrix products, arithmetic and copies ran while one was open for 6% of the time, Pallas kernels for 0%

profile of v1, /device:TPU:0, one launch (start us, length us, event | category | flops | bytes accessed | tf_op | source)
XLA Modules:
  0.0 819.6 jit_solution(14661528217365656713)
XLA Ops:
  14.3 13.1 %all-reduce.3 = (s32[192]{0:T(256)S(1)}, s32[192]{0:T(256)S(1)}, s32[192]{0:T(256)S(1)}) all-reduce(s32[192]{0:T(256)S(1)} %dynamic-update-slice.1, s32[192]{0:T(256)S(1)} %dynamic-update-slice, s32[192]{0:T(256)S(1)} %dynamic-update-slice.2), channel_id=1, replica_groups=mesh['lat'=4,'lon'=8] {'lon'}, use_global_device_ids=true, to_apply=%add.1 | all-reduce | flops 576 | bytes 4608
  29.1 4.6 copy_bitcast_fusion
  33.7 5.1 gather_fusion
  38.8 6.1 copy.96
  45.0 10.8 %gather.11 = bf16[8,3,78848]{2,1,0:T(4,128)(2,1)} reshape(bf16[24,128,616]{2,1,0:T(8,128)(2,1)} %copy.96) | data formatting | bytes 7569408 | tf_op jit(solution)/shard_map/jit(_take)/gather | solution.py:110
  55.7 7.2 select_select_fusion
  62.9 4.8 all-to-all-start
  69.8 2.9 collective-permute-start.5
  72.9 2.1 fusion.41
  75.7 76.7 %collective-permute-done.4 = bf16[24,1,512]{2,1,0:T(2,128)(2,1)S(1)} collective-permute-done((bf16[24,1,512]{2,1,0:T(2,128)(2,1)S(1)}, bf16[24,1,512]{2,1,0:T(2,128)(2,1)S(1)}, u32[]{:S(2)}, u32[]{:S(2)}) %collective-permute-start.4) | collective-permute-done | bytes 24608 | tf_op jit(solution)/shard_map/ppermute | solution.py:29
  153.8 3.2 collective-permute-start.7
  160.2 2.3 fusion.96
  170.0 2.7 convolution_add_fusion
  172.7 4.4 all-to-all-done
  177.1 10.8 %reshape.259 = bf16[3072,616]{1,0:T(8,128)(2,1)} reshape(bf16[8,3,78848]{2,1,0:T(4,128)(2,1)} %all-to-all-done) | data formatting | bytes 7569408 | tf_op jit(solution)/shard_map/reshape | solution.py:115
  187.9 7.0 multiply_convert_fusion
  195.9 6.3 fusion.1
  209.0 4.7 fusion.7
  217.3 2.9 collective-permute-start.1
  220.2 3.9 gather_fusion.1
  224.1 2.9 fusion.14
  227.1 4.5 fusion
  231.5 3.2 fusion.102
  238.5 2.4 collective-permute-done.3
  252.3 3.7 copy-done.18
  256.1 353.5 %all-reduce.9.cloned.1.call-done = (f32[3,3,512,512]{3,2,1,0:T(8,128)}, f32[616,512]{1,0:T(8,128)}) async-done(((f32[3,3,512,512]{3,2,1,0:T(8,128)}, f32[616,512]{1,0:T(8,128)}), (f32[3,3,512,512]{3,2,1,0:T(8,128)}, f32[616,512]{1,0:T(8,128)})) %all-reduce.9.cloned.1.call-update) | async-done | bytes 10698768 | tf_op jit(solution)/shard_map/psum | solution.py:15
  612.1 2.3 fusion.9
  614.5 19.2 %psum.46 = f32[512]{0:T(512)S(1)} all-reduce(f32[512]{0:T(512)S(1)} %fusion.9), channel_id=1, replica_groups=mesh['lat'=4,'lon'=8] {'lon'}, use_global_device_ids=true, to_apply=%region_16.17 | all-reduce | flops 512 | bytes 4096 | tf_op jit(solution)/shard_map/psum | solution.py:15
  633.7 6.7 psum.47
  640.9 2.2 fusion.43
  655.9 146.2 %all-reduce.11.cloned.1.call-done = (f32[3,3,512,512]{3,2,1,0:T(8,128)}, f32[616,512]{1,0:T(8,128)}) async-done(((f32[3,3,512,512]{3,2,1,0:T(8,128)}, f32[616,512]{1,0:T(8,128)}), (f32[3,3,512,512]{3,2,1,0:T(8,128)}, f32[616,512]{1,0:T(8,128)})) %all-reduce.11.cloned.1.call-update) | async-done | bytes 10698768 | tf_op jit(solution)/shard_map/psum | solution.py:15
  802.1 9.2 %broadcast_multiply_fusion = f32[3,3,512,512]{3,2,1,0:T(8,128)} fusion(f32[3,3,512,512]{3,2,1,0:T(8,128)} %get-tuple-element.14), kind=kLoop, calls=%fused_computation.11 | loop fusion | flops 2359296 | bytes 18874368 | tf_op jit(solution)/shard_map/mul | solution.py:187
  (153 shorter events, 66.3 us)
Async XLA Ops:
  7.2 180.7 %copy-start = (bf16[616,512]{1,0:T(8,128)(2,1)S(1)}, bf16[616,512]{1,0:T(8,128)(2,1)}, u32[]{:S(2)}) copy-start(bf16[616,512]{1,0:T(8,128)(2,1)} %param.13) | copy-start | bytes 1892356
  62.9 4.8 copy-start.2
  62.9 114.1 %all-to-all-start = ((bf16[8,3,78848]{2,1,0:T(4,128)(2,1)}), bf16[8,3,78848]{2,1,0:T(4,128)(2,1)}, u32[]{:S(2)}, u32[]{:S(2)}) async-start(bf16[8,3,78848]{2,1,0:T(4,128)(2,1)} %select_select_fusion), calls=%async_computation | async-start | bytes 10092544 | tf_op jit(solution)/shard_map/all_to_all | solution.py:112
  67.7 541.9 %all-reduce.9.cloned.1.call-start = ((), (), s32[]{:S(2)}) async-start(), calls=%async_computation.1 | async-start | bytes 21397504 | tf_op jit(solution)/shard_map/psum | solution.py:15
  67.9 84.6 %collective-permute-start.4 = (bf16[24,1,512]{2,1,0:T(2,128)(2,1)S(1)}, bf16[24,1,512]{2,1,0:T(2,128)(2,1)S(1)}, u32[]{:S(2)}, u32[]{:S(2)}) collective-permute-start(bf16[24,1,512]{2,1,0:T(2,128)(2,1)S(1)} %get-tuple-element.44), channel_id=1, source_target_pairs={{0,1},{1,2},{2,3},{3,4},{4,5},{5,6},{6,7},{7,0},{8,9},{9,10},{10,1... | collective-permute-start | bytes 73736 | tf_op jit(solution)/shard_map/ppermute | solution.py:29
  69.8 82.7 %collective-permute-start.5 = (bf16[24,1,512]{2,1,0:T(2,128)(2,1)S(1)}, bf16[24,1,512]{2,1,0:T(2,128)(2,1)S(1)}, u32[]{:S(2)}, u32[]{:S(2)}) collective-permute-start(bf16[24,1,512]{2,1,0:T(2,128)(2,1)S(1)} %get-tuple-element.45), channel_id=1, source_target_pairs={{1,0},{2,1},{3,2},{4,3},{5,4},{6,5},{7,6},{0,7},{9,8},{10,9},{11,1... | collective-permute-start | bytes 73736 | tf_op jit(solution)/shard_map/ppermute | solution.py:30
  72.9 2.2 copy-start.20
  152.5 5.6 collective-permute-start.6
  153.8 4.3 collective-permute-start.7
  158.1 4.4 slice-start
  160.1 2.4 slice-start.1
  204.1 3.2 copy-start.3
  204.1 4.2 copy-start.4
  204.1 4.2 copy-start.21
  209.0 4.7 copy-start.11
  215.3 19.5 %collective-permute-start = (bf16[24,1,512]{2,1,0:T(2,128)(2,1)S(1)}, bf16[24,1,512]{2,1,0:T(2,128)(2,1)S(1)}, u32[]{:S(2)}, u32[]{:S(2)}) collective-permute-start(bf16[24,1,512]{2,1,0:T(2,128)(2,1)S(1)} %get-tuple-element.40), channel_id=1, source_target_pairs={{0,1},{1,2},{2,3},{3,4},{4,5},{5,6},{6,7},{7,0},{8,9},{9,10},{10,1... | collective-permute-start | bytes 73736 | tf_op jit(solution)/shard_map/ppermute | solution.py:29
  217.3 17.4 %collective-permute-start.1 = (bf16[24,1,512]{2,1,0:T(2,128)(2,1)S(1)}, bf16[24,1,512]{2,1,0:T(2,128)(2,1)S(1)}, u32[]{:S(2)}, u32[]{:S(2)}) collective-permute-start(bf16[24,1,512]{2,1,0:T(2,128)(2,1)S(1)} %get-tuple-element.41), channel_id=1, source_target_pairs={{1,0},{2,1},{3,2},{4,3},{5,4},{6,5},{7,6},{0,7},{9,8},{10,9},{11,1... | collective-permute-start | bytes 73736 | tf_op jit(solution)/shard_map/ppermute | solution.py:30
  227.1 4.5 copy-start.10
  231.5 3.2 copy-start.7
  234.8 3.7 collective-permute-start.2
  236.1 4.9 collective-permute-start.3
  238.5 7.6 copy-start.16
  238.5 9.6 %copy-start.14 = (bf16[24,64,512]{2,1,0:T(8,128)(2,1)}, bf16[24,64,512]{2,1,0:T(8,128)(2,1)S(1)}, u32[]{:S(2)}) copy-start(bf16[24,64,512]{2,1,0:T(8,128)(2,1)S(1)} %get-tuple-element.38) | copy-start | bytes 4718596
  243.0 2.1 copy-start.12
  243.0 8.2 copy-start.8
  252.3 3.7 copy-start.18
  256.0 546.1 %all-reduce.11.cloned.1.call-start = ((), (), s32[]{:S(2)}) async-start(), calls=%async_computation.2 | async-start | bytes 21397504 | tf_op jit(solution)/shard_map/psum | solution.py:15
  609.7 2.4 copy-start.5
  640.9 2.2 copy-start.13
  640.9 3.3 slice-start.2
  802.1 9.2 %copy-start.19 = (f32[616,512]{1,0:T(8,128)S(1)}, f32[616,512]{1,0:T(8,128)}, u32[]{:S(2)}) copy-start(f32[616,512]{1,0:T(8,128)} %get-tuple-element.15) | copy-start | bytes 3784708
  802.1 10.4 %copy-start.1 = (bf16[616,512]{1,0:T(8,128)(2,1)S(1)}, bf16[616,512]{1,0:T(8,128)(2,1)}, u32[]{:S(2)}) copy-start(bf16[616,512]{1,0:T(8,128)(2,1)} %param.13) | copy-start | bytes 1892356
  (5 other events, 6.7 us)
Sparse Core Ops, SparseCore 0:
  256.1 353.4 all-reduce.8
  612.2 189.8 all-reduce.10
